TPU v7x, 32 devices: a whole 2x2x4 slice. The times are simulated.
32 devices in a mesh: gx: 4 (over z), gy: 2 (over core), gz: 4 (over y, x).
Axes of the slice: x: 2, y: 2, z: 4, core: 2. Of those that a mesh axis runs over, the one named last changes fastest.
Arguments:
- e_field: float32 [3, 16, 32, 512], P(None, 'gx', 'gy', 'gz'), may hold values from -6 to 6
- h_field: float32 [3, 16, 32, 512], P(None, 'gx', 'gy', 'gz'), may hold values from -6 to 6
- current: float32 [3, 16, 32, 512], P(None, 'gx', 'gy', 'gz'), may hold values from -6 to 6
- material: int32 [16, 32, 512], P('gx', 'gy', 'gz'), may hold values from 0 to 2
- sigma_table: float32 [3], replicated, may hold values from 0.05 to 2
- gamma_table: float32 [3], replicated, may hold values from 0.05 to 1
- plasma_table: float32 [3], replicated, may hold values from 0.3 to 2
- g_kernel: float32 [4], replicated, may hold values from -4 to 4
- surf_cell: int32 [4, 2, 4, 1024], P('gx', 'gy', 'gz'), may hold values from 0 to 8191
- surf_owner: int32 [4, 2, 4, 1024, 1], P('gx', 'gy', 'gz'), may hold values from 0 to 7; in each aligned block of 1024 rows (0 to 1023, 1024 to 2047, ..., all dimensions but the last counted through in order) at most 192 rows name the same one
- surf_tile: int32 [4, 2, 4, 1024], P('gx', 'gy', 'gz'), may hold values from 0 to 127
- surf_normal: int32 [4, 2, 4, 1024], P('gx', 'gy', 'gz'), may hold values from 0 to 5
- row_count: int32 [4, 2, 4], P('gx', 'gy', 'gz'), may hold values from 256 to 1024, as said below
Outputs:
- e_out: float32 [3, 16, 32, 512], P(None, 'gx', 'gy', 'gz')
- h_out: float32 [3, 16, 32, 512], P(None, 'gx', 'gy', 'gz')
- force: float32 [3, 4096], P(None, ('gx', 'gy', 'gz'))
Inputs may be any that keep to these rules, and one draw needn't show every extreme that they name: `surf_owner`: among the slots of one device no owner is named more than 192 times, a bound that some block reaches. `row_count`: some brick has all 1024 slots live.
All inputs are finite; a program needn't handle non-finite values.
Results may differ from a plain program's by a relative error of at most 0.00019.
Values sent between devices are 32-bit elements; how exact they have to be, the bound alone decides.
No kernel may reach another device: no remote copies, remote signals or barrier semaphores. Data moves between devices by JAX's collectives and lax.ppermute only.
A program may use at most 64 MiB of HBM per device.

v0:
```python
import jax
import jax.numpy as jnp
from jax import lax
from jax.sharding import PartitionSpec as P

TILE_DEV = 128
STEP_DT = 0.5
FACE_AREA = 0.25


def passed_along(shard, axis, by):
    peers = lax.axis_size(axis)
    pairs = [(i, i + by) for i in range(peers) if 0 <= i + by < peers]
    return lax.ppermute(shard, axis, pairs)


def lookup(material, table):
    result = jnp.zeros(material.shape, table.dtype)
    for which in range(table.shape[0]):
        result = result + jnp.where(material == which, table[which], jnp.zeros((), table.dtype))
    return result


def coefficients(material, sigma_table, gamma_table, plasma_table):
    sigma = lookup(material, sigma_table)
    gamma = lookup(material, gamma_table)
    plasma = lookup(material, plasma_table)
    keep_e = (1.0 - sigma * STEP_DT / 2) / (1.0 + sigma * STEP_DT / 2)
    gain_e = STEP_DT / (1.0 + sigma * STEP_DT / 2)
    keep_j = (1.0 - gamma * STEP_DT / 2) / (1.0 + gamma * STEP_DT / 2)
    gain_j = plasma * STEP_DT / (1.0 + gamma * STEP_DT / 2)
    return (keep_e, gain_e, keep_j, gain_j)


def row_forces(elec_rows, magn_rows, normal):
    axis_of = normal // 2
    sign_of = (1 - 2 * (normal % 2)).astype(elec_rows.dtype)
    picked = (axis_of[None, :] == jnp.arange(3, dtype=jnp.int32)[:, None]).astype(elec_rows.dtype)
    elec_n = jnp.sum(elec_rows * picked, axis=0)
    magn_n = jnp.sum(magn_rows * picked, axis=0)
    energy = 0.5 * (jnp.sum(elec_rows * elec_rows, axis=0) + jnp.sum(magn_rows * magn_rows, axis=0))
    return sign_of * (elec_rows * elec_n + magn_rows * magn_n - picked * energy)


def curl_upper(electric):
    rim_x = passed_along(electric[1:3, :1], "gx", -1)
    rim_y = passed_along(electric[0::2, :, :1], "gy", -1)
    rim_z = passed_along(electric[0:2, :, :, :1], "gz", -1)
    elec_x, elec_y, elec_z = (electric[0], electric[1], electric[2])
    y_next_x = jnp.concatenate([elec_y[1:], rim_x[0]], 0)
    z_next_x = jnp.concatenate([elec_z[1:], rim_x[1]], 0)
    x_next_y = jnp.concatenate([elec_x[:, 1:], rim_y[0]], 1)
    z_next_y = jnp.concatenate([elec_z[:, 1:], rim_y[1]], 1)
    x_next_z = jnp.concatenate([elec_x[:, :, 1:], rim_z[0]], 2)
    y_next_z = jnp.concatenate([elec_y[:, :, 1:], rim_z[1]], 2)
    curl_x = z_next_y - elec_z - (y_next_z - elec_y)
    curl_y = x_next_z - elec_x - (z_next_x - elec_z)
    curl_z = y_next_x - elec_y - (x_next_y - elec_x)
    return jnp.stack([curl_x, curl_y, curl_z])


def curl_lower(magnetic):
    rim_x = passed_along(magnetic[1:3, -1:], "gx", 1)
    rim_y = passed_along(magnetic[0::2, :, -1:], "gy", 1)
    rim_z = passed_along(magnetic[0:2, :, :, -1:], "gz", 1)
    magn_x, magn_y, magn_z = (magnetic[0], magnetic[1], magnetic[2])
    y_prev_x = jnp.concatenate([rim_x[0], magn_y[:-1]], 0)
    z_prev_x = jnp.concatenate([rim_x[1], magn_z[:-1]], 0)
    x_prev_y = jnp.concatenate([rim_y[0], magn_x[:, :-1]], 1)
    z_prev_y = jnp.concatenate([rim_y[1], magn_z[:, :-1]], 1)
    x_prev_z = jnp.concatenate([rim_z[0], magn_x[:, :, :-1]], 2)
    y_prev_z = jnp.concatenate([rim_z[1], magn_y[:, :, :-1]], 2)
    curl_x = magn_z - z_prev_y - (magn_y - y_prev_z)
    curl_y = magn_x - x_prev_z - (magn_z - z_prev_x)
    curl_z = magn_y - y_prev_x - (magn_x - x_prev_y)
    return jnp.stack([curl_x, curl_y, curl_z])


def local(
    e_field,
    h_field,
    current,
    material,
    sigma_table,
    gamma_table,
    plasma_table,
    g_kernel,
    surf_cell,
    surf_owner,
    surf_tile,
    surf_normal,
    row_count,
):
    keep_e, gain_e, keep_j, gain_j = coefficients(material, sigma_table, gamma_table, plasma_table)
    electric, magnetic, drude = (e_field, h_field, current)
    slot_cells = surf_cell.reshape(-1)
    normal = surf_normal.reshape(-1)
    owners = surf_owner.reshape(-1)
    tile_ids = surf_tile.reshape(-1)
    slot_total = slot_cells.shape[0]
    live_mask = (jnp.arange(slot_total, dtype=jnp.int32) < row_count.reshape(())).astype(
        jnp.float32
    )
    summed = jnp.zeros((3, slot_total), jnp.float32)
    for moment in range(g_kernel.shape[0]):
        magnetic = magnetic - STEP_DT * curl_upper(electric)
        curl_magn = curl_lower(magnetic)
        drude = keep_j * drude + gain_j * electric
        electric = keep_e * electric + gain_e * (curl_magn - drude)
        elec_rows = electric.reshape(3, -1)[:, slot_cells]
        magn_rows = magnetic.reshape(3, -1)[:, slot_cells]
        summed = summed + g_kernel[moment] * row_forces(elec_rows, magn_rows, normal)
    row_force = FACE_AREA * summed * live_mask
    groups = lax.axis_size("gx") * lax.axis_size("gy")
    capacity = 3 * slot_total // (2 * groups)
    owner_hot = (owners[:, None] == jnp.arange(groups, dtype=jnp.int32)[None, :]).astype(jnp.int32)
    ranks = jnp.sum(jnp.cumsum(owner_hot, axis=0) * owner_hot, axis=1) - 1
    force_buf = jnp.zeros((3, capacity, groups), jnp.float32).at[:, ranks, owners].set(row_force)
    tile_buf = (
        jnp.full((1, capacity, groups), -1.0, jnp.float32)
        .at[0, ranks, owners]
        .set(tile_ids.astype(jnp.float32))
    )
    got_force, got_tile = (
        lax.all_to_all(force_buf, ("gx", "gy"), split_axis=2, concat_axis=2, tiled=True),
        lax.all_to_all(tile_buf, ("gx", "gy"), split_axis=2, concat_axis=2, tiled=True),
    )
    tile_hot = (
        got_tile[0][:, :, None] == jnp.arange(TILE_DEV, dtype=jnp.float32)[None, None, :]
    ).astype(jnp.float32)
    force = jnp.einsum("acs,cst->at", got_force, tile_hot, precision=lax.Precision.HIGHEST)
    return (electric, magnetic, force)


def solution(mesh):
    return jax.shard_map(
        local,
        mesh=mesh,
        in_specs=(
            P(None, "gx", "gy", "gz"),
            P(None, "gx", "gy", "gz"),
            P(None, "gx", "gy", "gz"),
            P("gx", "gy", "gz"),
            P(),
            P(),
            P(),
            P(),
            P("gx", "gy", "gz", None),
            P("gx", "gy", "gz", None, None),
            P("gx", "gy", "gz", None),
            P("gx", "gy", "gz", None),
            P("gx", "gy", "gz"),
        ),
        out_specs=(
            P(None, "gx", "gy", "gz"),
            P(None, "gx", "gy", "gz"),
            P(None, ("gx", "gy", "gz")),
        ),
        check_vma=False,
    )
```

profile of v0, /device:TPU:0, one launch (start us, length us, event | category | flops | bytes accessed | tf_op | source)
XLA Modules:
  0.0 190.6 jit_solution(9184814041773252684)
XLA Ops:
  11.8 4.3 %scatter_custom_fusion.1 = f32[1536]{0:T(1024)S(1)} fusion(s32[1024]{0:T(1024)S(1)} %broadcast_select_fusion, f32[1024]{0:T(1024)S(1)} %bitcast.311, f32[]{:T(128)} %constant.91.clone.1), kind=kCustom, calls=%fused_computation.263 | custom fusion | bytes 6148
  16.8 7.9 %all-to-all-start.1 = ((f32[1,192,8]{1,0,2:T(1,128)}), f32[1,192,8]{1,0,2:T(1,128)S(1)}, u32[]{:S(2)}, u32[]{:S(2)}) async-start(f32[1,192,8]{1,0,2:T(1,128)} %bitcast.99), calls=%async_computation.1 | async-start | bytes 16384 | tf_op jit(solution)/shard_map/all_to_all | solution.py:126
  40.4 5.7 %add_divide_fusion = (f32[4,16,128]{2,1,0:T(8,128)S(1)}, f32[4,16,128]{2,1,0:T(8,128)S(1)}, f32[4,16,128]{2,1,0:T(8,128)S(1)}) fusion(pred[4,16,128]{2,1,0:T(8,128)(4,1)S(1)} %get-tuple-element.38, pred[4,16,128]{2,1,0:T(8,128)(4,1)S(1)} %get-tuple-element.37, pred[4,16,128]{2,1,0:T(8,128)(4,1)S(1)} %get-tuple-element.36, f32[]{:T(128)} %bitcast.2, ...), kind=kLoop, calls=%fused_computation.155 | loop fusion | flops 196608 | bytes 122916 | tf_op jit(solution)/shard_map/div | solution.py:29
  50.6 3.5 %collective-permute-start.5 = (f32[2,1,16,128]{3,2,1,0:T(8,128)S(1)}, f32[2,1,16,128]{3,2,1,0:T(8,128)S(1)}, u32[]{:S(2)}, u32[]{:S(2)}) collective-permute-start(f32[2,1,16,128]{3,2,1,0:T(8,128)S(1)} %slice.704), channel_id=1, source_target_pairs={{0,8},{8,16},{16,24},{1,9},{9,17},{17,25},{2,10},{10,18},{18,26},{... | collective-permute-start | bytes 49160 | tf_op jit(solution)/shard_map/ppermute | solution.py:14
  54.2 4.3 %collective-permute-start.4 = (f32[2,4,16,1]{3,2,1,0:T(8,128)S(1)}, f32[2,4,16,1]{3,2,1,0:T(8,128)S(1)}, u32[]{:S(2)}, u32[]{:S(2)}) collective-permute-start(f32[2,4,16,1]{3,2,1,0:T(8,128)S(1)} %slice.698), channel_id=1, source_target_pairs={{0,1},{1,2},{2,3},{4,5},{5,6},{6,7},{8,9},{9,10},{10,11},{12,13},{... | collective-permute-start | bytes 1544 | tf_op jit(solution)/shard_map/ppermute | solution.py:14
  61.1 5.0 %gather_fusion.1 = f32[1024,3]{1,0:T(8,128)S(1)} fusion(f32[3,8192]{0,1:T(8,128)} %bitcast.295, s32[1024]{0:T(1024)S(1)} %broadcast_clamp_fusion), kind=kCustom, calls=%fused_computation.1 | custom fusion | bytes 28672 | tf_op jit(solution)/shard_map/gather | solution.py:111
  73.3 5.0 %gather_fusion = f32[1024,3]{1,0:T(8,128)S(1)} fusion(f32[3,8192]{0,1:T(8,128)} %bitcast.296, s32[1024]{0:T(1024)S(1)} %broadcast_clamp_fusion), kind=kCustom, calls=%fused_computation | custom fusion | bytes 28672 | tf_op jit(solution)/shard_map/gather | solution.py:110
  78.9 3.0 %collective-permute-start.9 = (f32[2,4,1,128]{3,2,1,0:T(1,128)S(1)}, f32[2,4,1,128]{3,2,1,0:T(1,128)S(1)}, u32[]{:S(2)}, u32[]{:S(2)}) collective-permute-start(f32[2,4,1,128]{3,2,1,0:T(1,128)S(1)} %slice.573), channel_id=1, source_target_pairs={{0,4},{1,5},{2,6},{3,7},{8,12},{9,13},{10,14},{11,15},{16,20},{17,... | collective-permute-start | bytes 12296 | tf_op jit(solution)/shard_map/ppermute | solution.py:14
  81.9 4.3 %collective-permute-start.11 = (f32[2,1,16,128]{3,2,1,0:T(8,128)S(1)}, f32[2,1,16,128]{3,2,1,0:T(8,128)S(1)}, u32[]{:S(2)}, u32[]{:S(2)}) collective-permute-start(f32[2,1,16,128]{3,2,1,0:T(8,128)S(1)} %slice.738), channel_id=1, source_target_pairs={{0,8},{8,16},{16,24},{1,9},{9,17},{17,25},{2,10},{10,18},{18,26},{... | collective-permute-start | bytes 49160 | tf_op jit(solution)/shard_map/ppermute | solution.py:14
  86.2 4.9 %collective-permute-start.10 = (f32[2,4,16,1]{3,2,1,0:T(8,128)S(1)}, f32[2,4,16,1]{3,2,1,0:T(8,128)S(1)}, u32[]{:S(2)}, u32[]{:S(2)}) collective-permute-start(f32[2,4,16,1]{3,2,1,0:T(8,128)S(1)} %slice.732), channel_id=1, source_target_pairs={{0,1},{1,2},{2,3},{4,5},{5,6},{6,7},{8,9},{9,10},{10,11},{12,13},{... | collective-permute-start | bytes 1544 | tf_op jit(solution)/shard_map/ppermute | solution.py:14
  93.8 5.0 %gather_fusion.3 = f32[1024,3]{1,0:T(8,128)S(1)} fusion(f32[3,8192]{0,1:T(8,128)} %bitcast.297, s32[1024]{0:T(1024)S(1)} %broadcast_clamp_fusion), kind=kCustom, calls=%fused_computation.3 | custom fusion | bytes 28672 | tf_op jit(solution)/shard_map/gather | solution.py:111
  106.0 5.0 %gather_fusion.2 = f32[1024,3]{1,0:T(8,128)S(1)} fusion(f32[3,8192]{0,1:T(8,128)} %bitcast.298, s32[1024]{0:T(1024)S(1)} %broadcast_clamp_fusion), kind=kCustom, calls=%fused_computation.2 | custom fusion | bytes 28672 | tf_op jit(solution)/shard_map/gather | solution.py:110
  111.5 3.0 %collective-permute-start.15 = (f32[2,4,1,128]{3,2,1,0:T(1,128)S(1)}, f32[2,4,1,128]{3,2,1,0:T(1,128)S(1)}, u32[]{:S(2)}, u32[]{:S(2)}) collective-permute-start(f32[2,4,1,128]{3,2,1,0:T(1,128)S(1)} %slice.609), channel_id=1, source_target_pairs={{0,4},{1,5},{2,6},{3,7},{8,12},{9,13},{10,14},{11,15},{16,20},{17,... | collective-permute-start | bytes 12296 | tf_op jit(solution)/shard_map/ppermute | solution.py:14
  114.5 4.3 %collective-permute-start.17 = (f32[2,1,16,128]{3,2,1,0:T(8,128)S(1)}, f32[2,1,16,128]{3,2,1,0:T(8,128)S(1)}, u32[]{:S(2)}, u32[]{:S(2)}) collective-permute-start(f32[2,1,16,128]{3,2,1,0:T(8,128)S(1)} %slice.772), channel_id=1, source_target_pairs={{0,8},{8,16},{16,24},{1,9},{9,17},{17,25},{2,10},{10,18},{18,26},{... | collective-permute-start | bytes 49160 | tf_op jit(solution)/shard_map/ppermute | solution.py:14
  118.8 5.2 %collective-permute-start.16 = (f32[2,4,16,1]{3,2,1,0:T(8,128)S(1)}, f32[2,4,16,1]{3,2,1,0:T(8,128)S(1)}, u32[]{:S(2)}, u32[]{:S(2)}) collective-permute-start(f32[2,4,16,1]{3,2,1,0:T(8,128)S(1)} %slice.766), channel_id=1, source_target_pairs={{0,1},{1,2},{2,3},{4,5},{5,6},{6,7},{8,9},{9,10},{10,11},{12,13},{... | collective-permute-start | bytes 1544 | tf_op jit(solution)/shard_map/ppermute | solution.py:14
  126.6 5.0 %gather_fusion.5 = f32[1024,3]{1,0:T(8,128)S(1)} fusion(f32[3,8192]{0,1:T(8,128)} %bitcast.299, s32[1024]{0:T(1024)S(1)} %broadcast_clamp_fusion), kind=kCustom, calls=%fused_computation.5 | custom fusion | bytes 28672 | tf_op jit(solution)/shard_map/gather | solution.py:111
  138.8 5.0 %gather_fusion.4 = f32[1024,3]{1,0:T(8,128)S(1)} fusion(f32[3,8192]{0,1:T(8,128)} %bitcast.300, s32[1024]{0:T(1024)S(1)} %broadcast_clamp_fusion), kind=kCustom, calls=%fused_computation.4 | custom fusion | bytes 28672 | tf_op jit(solution)/shard_map/gather | solution.py:110
  147.4 4.3 %collective-permute-start.23 = (f32[2,1,16,128]{3,2,1,0:T(8,128)S(1)}, f32[2,1,16,128]{3,2,1,0:T(8,128)S(1)}, u32[]{:S(2)}, u32[]{:S(2)}) collective-permute-start(f32[2,1,16,128]{3,2,1,0:T(8,128)S(1)} %slice.806), channel_id=1, source_target_pairs={{0,8},{8,16},{16,24},{1,9},{9,17},{17,25},{2,10},{10,18},{18,26},{... | collective-permute-start | bytes 49160 | tf_op jit(solution)/shard_map/ppermute | solution.py:14
  151.7 5.2 %collective-permute-start.22 = (f32[2,4,16,1]{3,2,1,0:T(8,128)S(1)}, f32[2,4,16,1]{3,2,1,0:T(8,128)S(1)}, u32[]{:S(2)}, u32[]{:S(2)}) collective-permute-start(f32[2,4,16,1]{3,2,1,0:T(8,128)S(1)} %slice.800), channel_id=1, source_target_pairs={{0,1},{1,2},{2,3},{4,5},{5,6},{6,7},{8,9},{9,10},{10,11},{12,13},{... | collective-permute-start | bytes 1544 | tf_op jit(solution)/shard_map/ppermute | solution.py:14
  159.5 5.0 %gather_fusion.7 = f32[1024,3]{1,0:T(8,128)S(1)} fusion(f32[3,8192]{0,1:T(8,128)} %bitcast.301, s32[1024]{0:T(1024)S(1)} %broadcast_clamp_fusion), kind=kCustom, calls=%fused_computation.7 | custom fusion | bytes 28672 | tf_op jit(solution)/shard_map/gather | solution.py:111
  167.6 5.0 %gather_fusion.6 = f32[1024,3]{1,0:T(8,128)S(1)} fusion(f32[3,8192]{0,1:T(8,128)} %bitcast.294, s32[1024]{0:T(1024)S(1)} %broadcast_clamp_fusion), kind=kCustom, calls=%fused_computation.6 | custom fusion | bytes 28672 | tf_op jit(solution)/shard_map/gather | solution.py:110
  175.9 3.3 %scatter_custom_fusion = f32[3,1536]{0,1:T(8,128)S(1)} fusion(s32[1024]{0:T(1024)S(1)} %broadcast_select_fusion.1, f32[1024,3]{1,0:T(8,128)S(1)} %copy.60, f32[]{:T(128)} %constant.82.clone.1), kind=kCustom, calls=%fused_computation.12 | custom fusion | bytes 18436
  180.2 3.6 %all-to-all-start = ((f32[3,192,8]{1,0,2:T(4,128)}), f32[3,192,8]{1,0,2:T(4,128)S(1)}, u32[]{:S(2)}, u32[]{:S(2)}) async-start(f32[3,192,8]{1,0,2:T(4,128)} %bitcast.97), calls=%async_computation | async-start | bytes 65536 | tf_op jit(solution)/shard_map/all_to_all | solution.py:125
  183.8 5.7 %all-to-all-done = f32[3,192,8]{1,0,2:T(4,128)S(1)} async-done(((f32[3,192,8]{1,0,2:T(4,128)}), f32[3,192,8]{1,0,2:T(4,128)S(1)}, u32[]{:S(2)}, u32[]{:S(2)}) %all-to-all-start) | async-done | bytes 18464 | tf_op jit(solution)/shard_map/all_to_all | solution.py:125
  (211 shorter events, 75.6 us)
Async XLA Ops:
  1.4 44.8 %collective-permute-start = (f32[2,4,1,128]{3,2,1,0:T(1,128)S(1)}, f32[2,4,1,128]{3,2,1,0:T(1,128)S(1)}, u32[]{:S(2)}, u32[]{:S(2)}) collective-permute-start(f32[2,4,1,128]{3,2,1,0:T(1,128)S(1)} %slice.514), channel_id=1, source_target_pairs={{4,0},{5,1},{6,2},{7,3},{12,8},{13,9},{14,10},{15,11},{20,16},{21,... | collective-permute-start | bytes 12296 | tf_op jit(solution)/shard_map/ppermute | solution.py:14
  3.4 42.8 %collective-permute-start.2 = (f32[2,1,16,128]{3,2,1,0:T(8,128)S(1)}, f32[2,1,16,128]{3,2,1,0:T(8,128)S(1)}, u32[]{:S(2)}, u32[]{:S(2)}) collective-permute-start(f32[2,1,16,128]{3,2,1,0:T(8,128)S(1)} %slice.524), channel_id=1, source_target_pairs={{8,0},{16,8},{24,16},{9,1},{17,9},{25,17},{10,2},{18,10},{26,18},{... | collective-permute-start | bytes 49160 | tf_op jit(solution)/shard_map/ppermute | solution.py:14
  16.8 163.3 %all-to-all-start.1 = ((f32[1,192,8]{1,0,2:T(1,128)}), f32[1,192,8]{1,0,2:T(1,128)S(1)}, u32[]{:S(2)}, u32[]{:S(2)}) async-start(f32[1,192,8]{1,0,2:T(1,128)} %bitcast.99), calls=%async_computation.1 | async-start | bytes 16384 | tf_op jit(solution)/shard_map/all_to_all | solution.py:126
  25.6 20.6 %collective-permute-start.1 = (f32[2,4,16,1]{3,2,1,0:T(8,128)S(1)}, f32[2,4,16,1]{3,2,1,0:T(8,128)S(1)}, u32[]{:S(2)}, u32[]{:S(2)}) collective-permute-start(f32[2,4,16,1]{3,2,1,0:T(8,128)S(1)} %slice.518), channel_id=1, source_target_pairs={{1,0},{2,1},{3,2},{5,4},{6,5},{7,6},{9,8},{10,9},{11,10},{13,12},{... | collective-permute-start | bytes 1544 | tf_op jit(solution)/shard_map/ppermute | solution.py:14
  48.2 18.1 %collective-permute-start.3 = (f32[2,4,1,128]{3,2,1,0:T(1,128)S(1)}, f32[2,4,1,128]{3,2,1,0:T(1,128)S(1)}, u32[]{:S(2)}, u32[]{:S(2)}) collective-permute-start(f32[2,4,1,128]{3,2,1,0:T(1,128)S(1)} %slice.531), channel_id=1, source_target_pairs={{0,4},{1,5},{2,6},{3,7},{8,12},{9,13},{10,14},{11,15},{16,20},{17,... | collective-permute-start | bytes 12296 | tf_op jit(solution)/shard_map/ppermute | solution.py:14
  50.6 15.7 %collective-permute-start.5 = (f32[2,1,16,128]{3,2,1,0:T(8,128)S(1)}, f32[2,1,16,128]{3,2,1,0:T(8,128)S(1)}, u32[]{:S(2)}, u32[]{:S(2)}) collective-permute-start(f32[2,1,16,128]{3,2,1,0:T(8,128)S(1)} %slice.704), channel_id=1, source_target_pairs={{0,8},{8,16},{16,24},{1,9},{9,17},{17,25},{2,10},{10,18},{18,26},{... | collective-permute-start | bytes 49160 | tf_op jit(solution)/shard_map/ppermute | solution.py:14
  54.2 12.2 %collective-permute-start.4 = (f32[2,4,16,1]{3,2,1,0:T(8,128)S(1)}, f32[2,4,16,1]{3,2,1,0:T(8,128)S(1)}, u32[]{:S(2)}, u32[]{:S(2)}) collective-permute-start(f32[2,4,16,1]{3,2,1,0:T(8,128)S(1)} %slice.698), channel_id=1, source_target_pairs={{0,1},{1,2},{2,3},{4,5},{5,6},{6,7},{8,9},{9,10},{10,11},{12,13},{... | collective-permute-start | bytes 1544 | tf_op jit(solution)/shard_map/ppermute | solution.py:14
  66.7 11.8 %collective-permute-start.6 = (f32[2,4,1,128]{3,2,1,0:T(1,128)S(1)}, f32[2,4,1,128]{3,2,1,0:T(1,128)S(1)}, u32[]{:S(2)}, u32[]{:S(2)}) collective-permute-start(f32[2,4,1,128]{3,2,1,0:T(1,128)S(1)} %slice.556), channel_id=1, source_target_pairs={{4,0},{5,1},{6,2},{7,3},{12,8},{13,9},{14,10},{15,11},{20,16},{21,... | collective-permute-start | bytes 12296 | tf_op jit(solution)/shard_map/ppermute | solution.py:14
  68.0 10.6 %collective-permute-start.8 = (f32[2,1,16,128]{3,2,1,0:T(8,128)S(1)}, f32[2,1,16,128]{3,2,1,0:T(8,128)S(1)}, u32[]{:S(2)}, u32[]{:S(2)}) collective-permute-start(f32[2,1,16,128]{3,2,1,0:T(8,128)S(1)} %slice.722), channel_id=1, source_target_pairs={{8,0},{16,8},{24,16},{9,1},{17,9},{25,17},{10,2},{18,10},{26,18},{... | collective-permute-start | bytes 49160 | tf_op jit(solution)/shard_map/ppermute | solution.py:14
  69.3 9.2 %collective-permute-start.7 = (f32[2,4,16,1]{3,2,1,0:T(8,128)S(1)}, f32[2,4,16,1]{3,2,1,0:T(8,128)S(1)}, u32[]{:S(2)}, u32[]{:S(2)}) collective-permute-start(f32[2,4,16,1]{3,2,1,0:T(8,128)S(1)} %slice.716), channel_id=1, source_target_pairs={{1,0},{2,1},{3,2},{5,4},{6,5},{7,6},{9,8},{10,9},{11,10},{13,12},{... | collective-permute-start | bytes 1544 | tf_op jit(solution)/shard_map/ppermute | solution.py:14
  78.9 20.1 %collective-permute-start.9 = (f32[2,4,1,128]{3,2,1,0:T(1,128)S(1)}, f32[2,4,1,128]{3,2,1,0:T(1,128)S(1)}, u32[]{:S(2)}, u32[]{:S(2)}) collective-permute-start(f32[2,4,1,128]{3,2,1,0:T(1,128)S(1)} %slice.573), channel_id=1, source_target_pairs={{0,4},{1,5},{2,6},{3,7},{8,12},{9,13},{10,14},{11,15},{16,20},{17,... | collective-permute-start | bytes 12296 | tf_op jit(solution)/shard_map/ppermute | solution.py:14
  81.9 17.1 %collective-permute-start.11 = (f32[2,1,16,128]{3,2,1,0:T(8,128)S(1)}, f32[2,1,16,128]{3,2,1,0:T(8,128)S(1)}, u32[]{:S(2)}, u32[]{:S(2)}) collective-permute-start(f32[2,1,16,128]{3,2,1,0:T(8,128)S(1)} %slice.738), channel_id=1, source_target_pairs={{0,8},{8,16},{16,24},{1,9},{9,17},{17,25},{2,10},{10,18},{18,26},{... | collective-permute-start | bytes 49160 | tf_op jit(solution)/shard_map/ppermute | solution.py:14
  86.2 12.8 %collective-permute-start.10 = (f32[2,4,16,1]{3,2,1,0:T(8,128)S(1)}, f32[2,4,16,1]{3,2,1,0:T(8,128)S(1)}, u32[]{:S(2)}, u32[]{:S(2)}) collective-permute-start(f32[2,4,16,1]{3,2,1,0:T(8,128)S(1)} %slice.732), channel_id=1, source_target_pairs={{0,1},{1,2},{2,3},{4,5},{5,6},{6,7},{8,9},{9,10},{10,11},{12,13},{... | collective-permute-start | bytes 1544 | tf_op jit(solution)/shard_map/ppermute | solution.py:14
  99.3 11.8 %collective-permute-start.12 = (f32[2,4,1,128]{3,2,1,0:T(1,128)S(1)}, f32[2,4,1,128]{3,2,1,0:T(1,128)S(1)}, u32[]{:S(2)}, u32[]{:S(2)}) collective-permute-start(f32[2,4,1,128]{3,2,1,0:T(1,128)S(1)} %slice.592), channel_id=1, source_target_pairs={{4,0},{5,1},{6,2},{7,3},{12,8},{13,9},{14,10},{15,11},{20,16},{21,... | collective-permute-start | bytes 12296 | tf_op jit(solution)/shard_map/ppermute | solution.py:14
  100.6 10.6 %collective-permute-start.14 = (f32[2,1,16,128]{3,2,1,0:T(8,128)S(1)}, f32[2,1,16,128]{3,2,1,0:T(8,128)S(1)}, u32[]{:S(2)}, u32[]{:S(2)}) collective-permute-start(f32[2,1,16,128]{3,2,1,0:T(8,128)S(1)} %slice.756), channel_id=1, source_target_pairs={{8,0},{16,8},{24,16},{9,1},{17,9},{25,17},{10,2},{18,10},{26,18},{... | collective-permute-start | bytes 49160 | tf_op jit(solution)/shard_map/ppermute | solution.py:14
  111.5 20.4 %collective-permute-start.15 = (f32[2,4,1,128]{3,2,1,0:T(1,128)S(1)}, f32[2,4,1,128]{3,2,1,0:T(1,128)S(1)}, u32[]{:S(2)}, u32[]{:S(2)}) collective-permute-start(f32[2,4,1,128]{3,2,1,0:T(1,128)S(1)} %slice.609), channel_id=1, source_target_pairs={{0,4},{1,5},{2,6},{3,7},{8,12},{9,13},{10,14},{11,15},{16,20},{17,... | collective-permute-start | bytes 12296 | tf_op jit(solution)/shard_map/ppermute | solution.py:14
  114.5 17.3 %collective-permute-start.17 = (f32[2,1,16,128]{3,2,1,0:T(8,128)S(1)}, f32[2,1,16,128]{3,2,1,0:T(8,128)S(1)}, u32[]{:S(2)}, u32[]{:S(2)}) collective-permute-start(f32[2,1,16,128]{3,2,1,0:T(8,128)S(1)} %slice.772), channel_id=1, source_target_pairs={{0,8},{8,16},{16,24},{1,9},{9,17},{17,25},{2,10},{10,18},{18,26},{... | collective-permute-start | bytes 49160 | tf_op jit(solution)/shard_map/ppermute | solution.py:14
  118.8 13.0 %collective-permute-start.16 = (f32[2,4,16,1]{3,2,1,0:T(8,128)S(1)}, f32[2,4,16,1]{3,2,1,0:T(8,128)S(1)}, u32[]{:S(2)}, u32[]{:S(2)}) collective-permute-start(f32[2,4,16,1]{3,2,1,0:T(8,128)S(1)} %slice.766), channel_id=1, source_target_pairs={{0,1},{1,2},{2,3},{4,5},{5,6},{6,7},{8,9},{9,10},{10,11},{12,13},{... | collective-permute-start | bytes 1544 | tf_op jit(solution)/shard_map/ppermute | solution.py:14
  132.2 11.8 %collective-permute-start.18 = (f32[2,4,1,128]{3,2,1,0:T(1,128)S(1)}, f32[2,4,1,128]{3,2,1,0:T(1,128)S(1)}, u32[]{:S(2)}, u32[]{:S(2)}) collective-permute-start(f32[2,4,1,128]{3,2,1,0:T(1,128)S(1)} %slice.628), channel_id=1, source_target_pairs={{4,0},{5,1},{6,2},{7,3},{12,8},{13,9},{14,10},{15,11},{20,16},{21,... | collective-permute-start | bytes 12296 | tf_op jit(solution)/shard_map/ppermute | solution.py:14
  133.5 10.6 %collective-permute-start.20 = (f32[2,1,16,128]{3,2,1,0:T(8,128)S(1)}, f32[2,1,16,128]{3,2,1,0:T(8,128)S(1)}, u32[]{:S(2)}, u32[]{:S(2)}) collective-permute-start(f32[2,1,16,128]{3,2,1,0:T(8,128)S(1)} %slice.790), channel_id=1, source_target_pairs={{8,0},{16,8},{24,16},{9,1},{17,9},{25,17},{10,2},{18,10},{26,18},{... | collective-permute-start | bytes 49160 | tf_op jit(solution)/shard_map/ppermute | solution.py:14
  144.4 20.4 %collective-permute-start.21 = (f32[2,4,1,128]{3,2,1,0:T(1,128)S(1)}, f32[2,4,1,128]{3,2,1,0:T(1,128)S(1)}, u32[]{:S(2)}, u32[]{:S(2)}) collective-permute-start(f32[2,4,1,128]{3,2,1,0:T(1,128)S(1)} %slice.645), channel_id=1, source_target_pairs={{0,4},{1,5},{2,6},{3,7},{8,12},{9,13},{10,14},{11,15},{16,20},{17,... | collective-permute-start | bytes 12296 | tf_op jit(solution)/shard_map/ppermute | solution.py:14
  147.4 17.3 %collective-permute-start.23 = (f32[2,1,16,128]{3,2,1,0:T(8,128)S(1)}, f32[2,1,16,128]{3,2,1,0:T(8,128)S(1)}, u32[]{:S(2)}, u32[]{:S(2)}) collective-permute-start(f32[2,1,16,128]{3,2,1,0:T(8,128)S(1)} %slice.806), channel_id=1, source_target_pairs={{0,8},{8,16},{16,24},{1,9},{9,17},{17,25},{2,10},{10,18},{18,26},{... | collective-permute-start | bytes 49160 | tf_op jit(solution)/shard_map/ppermute | solution.py:14
  151.7 13.0 %collective-permute-start.22 = (f32[2,4,16,1]{3,2,1,0:T(8,128)S(1)}, f32[2,4,16,1]{3,2,1,0:T(8,128)S(1)}, u32[]{:S(2)}, u32[]{:S(2)}) collective-permute-start(f32[2,4,16,1]{3,2,1,0:T(8,128)S(1)} %slice.800), channel_id=1, source_target_pairs={{0,1},{1,2},{2,3},{4,5},{5,6},{6,7},{8,9},{9,10},{10,11},{12,13},{... | collective-permute-start | bytes 1544 | tf_op jit(solution)/shard_map/ppermute | solution.py:14
  180.2 9.4 %all-to-all-start = ((f32[3,192,8]{1,0,2:T(4,128)}), f32[3,192,8]{1,0,2:T(4,128)S(1)}, u32[]{:S(2)}, u32[]{:S(2)}) async-start(f32[3,192,8]{1,0,2:T(4,128)} %bitcast.97), calls=%async_computation | async-start | bytes 65536 | tf_op jit(solution)/shard_map/all_to_all | solution.py:125
  (7 other events, 168.7 us)
where the time goes:
time: 193 us; the launch traced here: 191 us
  local copies, waits for them, and re-layouts  83.1 us (43%)
  starting transfers between devices  74.3 us (38%)
  other arithmetic  23.8 us (12%)
  waiting for transfers between devices  5.8 us (3%)
  between operations  2.54 us (1%)
    ppermute x24, starting transfers between devices, passed_along(): return lax.ppermute(shard, axis, pairs)  62.8 us
    gather x8, local copies, waits for them, and re-layouts, local(): magn_rows = magnetic.reshape(3, -1)[:, slot_cells]  20.7 us
    gather x8, local copies, waits for them, and re-layouts, local(): elec_rows = electric.reshape(3, -1)[:, slot_cells]  20.7 us
    sub x4, local copies, waits for them, and re-layouts, local(): magnetic = magnetic - STEP_DT * curl_upper(electric)  10.5 us
    add x4, local copies, waits for them, and re-layouts, local(): electric = keep_e * electric + gain_e * (curl_magn - drude)  10.5 us
    unnamed x15, local copies, waits for them, and re-layouts  9.26 us
    all_to_all x1, starting transfers between devices, local(): lax.all_to_all(tile_buf, ('gx', 'gy'), split_axis=2, concat_axis=2, tiled...  7.86 us
    all_to_all x1, waiting for transfers between devices, local(): lax.all_to_all(force_buf, ('gx', 'gy'), split_axis=2, concat_axis=2, tile...  5.74 us
  transfers between devices with their start and end apart: 26, of which 1 were waited for; matrix products, arithmetic and copies ran while one was open for 56% of the time, Pallas kernels for 0%

commit v1 on v0

--- a/solution.py
+++ b/solution.py
@@ -1,3 +1,4 @@
+import functools
 import jax
 import jax.numpy as jnp
 from jax import lax
@@ -6,6 +7,18 @@
 TILE_DEV = 128
 STEP_DT = 0.5
 FACE_AREA = 0.25
+
+
+def report_wall_on(local_x, where_dim, ndim_at):
+    arr_now = lax.axis_size(("gx", "gy"))
+    answer = jnp.split(local_x, arr_now, axis=where_dim)
+    built = jnp.stack(answer, axis=0)
+    current_arr = lax.all_to_all(built, ("gx", "gy"), 0, 0)
+    now = jnp.concatenate(current_arr, axis=ndim_at)
+    return now
+
+
+read_the_roots = functools.partial(report_wall_on, where_dim=2, ndim_at=2)
 
 
 def passed_along(shard, axis, by):
@@ -122,7 +135,7 @@
         .set(tile_ids.astype(jnp.float32))
     )
     got_force, got_tile = (
-        lax.all_to_all(force_buf, ("gx", "gy"), split_axis=2, concat_axis=2, tiled=True),
+        read_the_roots(force_buf),
         lax.all_to_all(tile_buf, ("gx", "gy"), split_axis=2, concat_axis=2, tiled=True),
     )
     tile_hot = (

time: 193 us -> 197 us (1.021)
  local copies, waits for them, and re-layouts: 83.1 us -> 87.3 us
    unnamed x15 -> x22, local copies, waits for them, and re-layouts: 9.26 us -> 12.8 us
  transfers between devices with their start and end apart: 26 -> 26, of which waited for: 1 -> 1; matrix products, arithmetic and copies ran while one was open for 56% -> 57% of each run, Pallas kernels for 0% -> 0%
where the time goes in v1:
time: 197 us; the launch traced here: 195 us
  local copies, waits for them, and re-layouts  87.3 us (44%)
  starting transfers between devices  74.3 us (38%)
  other arithmetic  23.8 us (12%)
  waiting for transfers between devices  5.76 us (3%)
  between operations  2.54 us (1%)
    ppermute x24, starting transfers between devices, passed_along(): return lax.ppermute(shard, axis, pairs)  62.8 us
    gather x8, local copies, waits for them, and re-layouts, local(): magn_rows = magnetic.reshape(3, -1)[:, slot_cells]  20.7 us
    gather x8, local copies, waits for them, and re-layouts, local(): elec_rows = electric.reshape(3, -1)[:, slot_cells]  20.7 us
    unnamed x22, local copies, waits for them, and re-layouts  12.8 us
    sub x4, local copies, waits for them, and re-layouts, local(): magnetic = magnetic - STEP_DT * curl_upper(electric)  10.5 us
    add x4, local copies, waits for them, and re-layouts, local(): electric = keep_e * electric + gain_e * (curl_magn - drude)  10.5 us
    all_to_all x1, starting transfers between devices, local(): lax.all_to_all(tile_buf, ('gx', 'gy'), split_axis=2, concat_axis=2, tiled...  7.86 us
    div x1, other arithmetic, coefficients(): gain_e = STEP_DT / (1.0 + sigma * STEP_DT / 2)  5.73 us
  transfers between devices with their start and end apart: 26, of which 1 were waited for; matrix products, arithmetic and copies ran while one was open for 57% of the time, Pallas kernels for 0%

profile of v1, /device:TPU:0, one launch (start us, length us, event | category | flops | bytes accessed | tf_op | source)
XLA Modules:
  0.0 194.7 jit_solution(9833098334722205153)
XLA Ops:
  11.8 4.3 %scatter_custom_fusion.1 = f32[1536]{0:T(1024)S(1)} fusion(s32[1024]{0:T(1024)S(1)} %broadcast_select_fusion, f32[1024]{0:T(1024)S(1)} %bitcast.355, f32[]{:T(128)} %constant.91.clone.1), kind=kCustom, calls=%fused_computation.273 | custom fusion | bytes 6148
  16.8 7.9 %all-to-all-start.1 = ((f32[1,192,8]{1,0,2:T(1,128)}), f32[1,192,8]{1,0,2:T(1,128)S(1)}, u32[]{:S(2)}, u32[]{:S(2)}) async-start(f32[1,192,8]{1,0,2:T(1,128)} %bitcast.109), calls=%async_computation.1 | async-start | bytes 16384 | tf_op jit(solution)/shard_map/all_to_all | solution.py:139
  40.4 5.7 %add_divide_fusion = (f32[4,16,128]{2,1,0:T(8,128)S(1)}, f32[4,16,128]{2,1,0:T(8,128)S(1)}, f32[4,16,128]{2,1,0:T(8,128)S(1)}) fusion(pred[4,16,128]{2,1,0:T(8,128)(4,1)S(1)} %get-tuple-element.38, pred[4,16,128]{2,1,0:T(8,128)(4,1)S(1)} %get-tuple-element.37, pred[4,16,128]{2,1,0:T(8,128)(4,1)S(1)} %get-tuple-element.36, f32[]{:T(128)} %bitcast.2, ...), kind=kLoop, calls=%fused_computation.157 | loop fusion | flops 196608 | bytes 122916 | tf_op jit(solution)/shard_map/div | solution.py:42
  50.6 3.5 %collective-permute-start.5 = (f32[2,1,16,128]{3,2,1,0:T(8,128)S(1)}, f32[2,1,16,128]{3,2,1,0:T(8,128)S(1)}, u32[]{:S(2)}, u32[]{:S(2)}) collective-permute-start(f32[2,1,16,128]{3,2,1,0:T(8,128)S(1)} %slice.704), channel_id=1, source_target_pairs={{0,8},{8,16},{16,24},{1,9},{9,17},{17,25},{2,10},{10,18},{18,26},{... | collective-permute-start | bytes 49160 | tf_op jit(solution)/shard_map/ppermute | solution.py:27
  54.2 4.3 %collective-permute-start.4 = (f32[2,4,16,1]{3,2,1,0:T(8,128)S(1)}, f32[2,4,16,1]{3,2,1,0:T(8,128)S(1)}, u32[]{:S(2)}, u32[]{:S(2)}) collective-permute-start(f32[2,4,16,1]{3,2,1,0:T(8,128)S(1)} %slice.698), channel_id=1, source_target_pairs={{0,1},{1,2},{2,3},{4,5},{5,6},{6,7},{8,9},{9,10},{10,11},{12,13},{... | collective-permute-start | bytes 1544 | tf_op jit(solution)/shard_map/ppermute | solution.py:27
  61.1 5.0 %gather_fusion.1 = f32[1024,3]{1,0:T(8,128)S(1)} fusion(f32[3,8192]{0,1:T(8,128)} %bitcast.331, s32[1024]{0:T(1024)S(1)} %broadcast_clamp_fusion), kind=kCustom, calls=%fused_computation.1 | custom fusion | bytes 28672 | tf_op jit(solution)/shard_map/gather | solution.py:124
  73.3 5.0 %gather_fusion = f32[1024,3]{1,0:T(8,128)S(1)} fusion(f32[3,8192]{0,1:T(8,128)} %bitcast.332, s32[1024]{0:T(1024)S(1)} %broadcast_clamp_fusion), kind=kCustom, calls=%fused_computation | custom fusion | bytes 28672 | tf_op jit(solution)/shard_map/gather | solution.py:123
  78.9 3.0 %collective-permute-start.9 = (f32[2,4,1,128]{3,2,1,0:T(1,128)S(1)}, f32[2,4,1,128]{3,2,1,0:T(1,128)S(1)}, u32[]{:S(2)}, u32[]{:S(2)}) collective-permute-start(f32[2,4,1,128]{3,2,1,0:T(1,128)S(1)} %slice.573), channel_id=1, source_target_pairs={{0,4},{1,5},{2,6},{3,7},{8,12},{9,13},{10,14},{11,15},{16,20},{17,... | collective-permute-start | bytes 12296 | tf_op jit(solution)/shard_map/ppermute | solution.py:27
  81.9 4.3 %collective-permute-start.11 = (f32[2,1,16,128]{3,2,1,0:T(8,128)S(1)}, f32[2,1,16,128]{3,2,1,0:T(8,128)S(1)}, u32[]{:S(2)}, u32[]{:S(2)}) collective-permute-start(f32[2,1,16,128]{3,2,1,0:T(8,128)S(1)} %slice.738), channel_id=1, source_target_pairs={{0,8},{8,16},{16,24},{1,9},{9,17},{17,25},{2,10},{10,18},{18,26},{... | collective-permute-start | bytes 49160 | tf_op jit(solution)/shard_map/ppermute | solution.py:27
  86.2 4.9 %collective-permute-start.10 = (f32[2,4,16,1]{3,2,1,0:T(8,128)S(1)}, f32[2,4,16,1]{3,2,1,0:T(8,128)S(1)}, u32[]{:S(2)}, u32[]{:S(2)}) collective-permute-start(f32[2,4,16,1]{3,2,1,0:T(8,128)S(1)} %slice.732), channel_id=1, source_target_pairs={{0,1},{1,2},{2,3},{4,5},{5,6},{6,7},{8,9},{9,10},{10,11},{12,13},{... | collective-permute-start | bytes 1544 | tf_op jit(solution)/shard_map/ppermute | solution.py:27
  93.8 5.0 %gather_fusion.3 = f32[1024,3]{1,0:T(8,128)S(1)} fusion(f32[3,8192]{0,1:T(8,128)} %bitcast.333, s32[1024]{0:T(1024)S(1)} %broadcast_clamp_fusion), kind=kCustom, calls=%fused_computation.3 | custom fusion | bytes 28672 | tf_op jit(solution)/shard_map/gather | solution.py:124
  106.0 5.0 %gather_fusion.2 = f32[1024,3]{1,0:T(8,128)S(1)} fusion(f32[3,8192]{0,1:T(8,128)} %bitcast.334, s32[1024]{0:T(1024)S(1)} %broadcast_clamp_fusion), kind=kCustom, calls=%fused_computation.2 | custom fusion | bytes 28672 | tf_op jit(solution)/shard_map/gather | solution.py:123
  111.5 3.0 %collective-permute-start.15 = (f32[2,4,1,128]{3,2,1,0:T(1,128)S(1)}, f32[2,4,1,128]{3,2,1,0:T(1,128)S(1)}, u32[]{:S(2)}, u32[]{:S(2)}) collective-permute-start(f32[2,4,1,128]{3,2,1,0:T(1,128)S(1)} %slice.609), channel_id=1, source_target_pairs={{0,4},{1,5},{2,6},{3,7},{8,12},{9,13},{10,14},{11,15},{16,20},{17,... | collective-permute-start | bytes 12296 | tf_op jit(solution)/shard_map/ppermute | solution.py:27
  114.5 4.3 %collective-permute-start.17 = (f32[2,1,16,128]{3,2,1,0:T(8,128)S(1)}, f32[2,1,16,128]{3,2,1,0:T(8,128)S(1)}, u32[]{:S(2)}, u32[]{:S(2)}) collective-permute-start(f32[2,1,16,128]{3,2,1,0:T(8,128)S(1)} %slice.772), channel_id=1, source_target_pairs={{0,8},{8,16},{16,24},{1,9},{9,17},{17,25},{2,10},{10,18},{18,26},{... | collective-permute-start | bytes 49160 | tf_op jit(solution)/shard_map/ppermute | solution.py:27
  118.8 5.2 %collective-permute-start.16 = (f32[2,4,16,1]{3,2,1,0:T(8,128)S(1)}, f32[2,4,16,1]{3,2,1,0:T(8,128)S(1)}, u32[]{:S(2)}, u32[]{:S(2)}) collective-permute-start(f32[2,4,16,1]{3,2,1,0:T(8,128)S(1)} %slice.766), channel_id=1, source_target_pairs={{0,1},{1,2},{2,3},{4,5},{5,6},{6,7},{8,9},{9,10},{10,11},{12,13},{... | collective-permute-start | bytes 1544 | tf_op jit(solution)/shard_map/ppermute | solution.py:27
  126.6 5.0 %gather_fusion.5 = f32[1024,3]{1,0:T(8,128)S(1)} fusion(f32[3,8192]{0,1:T(8,128)} %bitcast.335, s32[1024]{0:T(1024)S(1)} %broadcast_clamp_fusion), kind=kCustom, calls=%fused_computation.5 | custom fusion | bytes 28672 | tf_op jit(solution)/shard_map/gather | solution.py:124
  138.8 5.0 %gather_fusion.4 = f32[1024,3]{1,0:T(8,128)S(1)} fusion(f32[3,8192]{0,1:T(8,128)} %bitcast.336, s32[1024]{0:T(1024)S(1)} %broadcast_clamp_fusion), kind=kCustom, calls=%fused_computation.4 | custom fusion | bytes 28672 | tf_op jit(solution)/shard_map/gather | solution.py:123
  147.4 4.3 %collective-permute-start.23 = (f32[2,1,16,128]{3,2,1,0:T(8,128)S(1)}, f32[2,1,16,128]{3,2,1,0:T(8,128)S(1)}, u32[]{:S(2)}, u32[]{:S(2)}) collective-permute-start(f32[2,1,16,128]{3,2,1,0:T(8,128)S(1)} %slice.806), channel_id=1, source_target_pairs={{0,8},{8,16},{16,24},{1,9},{9,17},{17,25},{2,10},{10,18},{18,26},{... | collective-permute-start | bytes 49160 | tf_op jit(solution)/shard_map/ppermute | solution.py:27
  151.7 5.2 %collective-permute-start.22 = (f32[2,4,16,1]{3,2,1,0:T(8,128)S(1)}, f32[2,4,16,1]{3,2,1,0:T(8,128)S(1)}, u32[]{:S(2)}, u32[]{:S(2)}) collective-permute-start(f32[2,4,16,1]{3,2,1,0:T(8,128)S(1)} %slice.800), channel_id=1, source_target_pairs={{0,1},{1,2},{2,3},{4,5},{5,6},{6,7},{8,9},{9,10},{10,11},{12,13},{... | collective-permute-start | bytes 1544 | tf_op jit(solution)/shard_map/ppermute | solution.py:27
  159.5 5.0 %gather_fusion.7 = f32[1024,3]{1,0:T(8,128)S(1)} fusion(f32[3,8192]{0,1:T(8,128)} %bitcast.337, s32[1024]{0:T(1024)S(1)} %broadcast_clamp_fusion), kind=kCustom, calls=%fused_computation.7 | custom fusion | bytes 28672 | tf_op jit(solution)/shard_map/gather | solution.py:124
  167.6 5.0 %gather_fusion.6 = f32[1024,3]{1,0:T(8,128)S(1)} fusion(f32[3,8192]{0,1:T(8,128)} %bitcast.330, s32[1024]{0:T(1024)S(1)} %broadcast_clamp_fusion), kind=kCustom, calls=%fused_computation.6 | custom fusion | bytes 28672 | tf_op jit(solution)/shard_map/gather | solution.py:123
  175.9 3.3 %scatter_custom_fusion = f32[3,1536]{0,1:T(8,128)S(1)} fusion(s32[1024]{0:T(1024)S(1)} %broadcast_select_fusion.1, f32[1024,3]{1,0:T(8,128)S(1)} %copy.74, f32[]{:T(128)} %constant.82.clone.1), kind=kCustom, calls=%fused_computation.12 | custom fusion | bytes 18436
  184.3 3.6 %all-to-all-start = ((f32[8,3,192,1]{2,3,1,0:T(1,128)}), f32[8,3,192,1]{2,3,1,0:T(1,128)S(1)}, u32[]{:S(2)}, u32[]{:S(2)}) async-start(f32[8,3,192,1]{2,3,1,0:T(1,128)} %constant_dynamic-update-slice_fusion), calls=%async_computation | async-start | bytes 49152 | tf_op jit(solution)/shard_map/all_to_all | solution.py:16
  187.9 5.7 %all-to-all-done = f32[8,3,192,1]{2,3,1,0:T(1,128)S(1)} async-done(((f32[8,3,192,1]{2,3,1,0:T(1,128)}), f32[8,3,192,1]{2,3,1,0:T(1,128)S(1)}, u32[]{:S(2)}, u32[]{:S(2)}) %all-to-all-start) | async-done | bytes 18464 | tf_op jit(solution)/shard_map/all_to_all | solution.py:16
  (219 shorter events, 79.8 us)
Async XLA Ops:
  1.4 44.8 %collective-permute-start = (f32[2,4,1,128]{3,2,1,0:T(1,128)S(1)}, f32[2,4,1,128]{3,2,1,0:T(1,128)S(1)}, u32[]{:S(2)}, u32[]{:S(2)}) collective-permute-start(f32[2,4,1,128]{3,2,1,0:T(1,128)S(1)} %slice.514), channel_id=1, source_target_pairs={{4,0},{5,1},{6,2},{7,3},{12,8},{13,9},{14,10},{15,11},{20,16},{21,... | collective-permute-start | bytes 12296 | tf_op jit(solution)/shard_map/ppermute | solution.py:27
  3.4 42.8 %collective-permute-start.2 = (f32[2,1,16,128]{3,2,1,0:T(8,128)S(1)}, f32[2,1,16,128]{3,2,1,0:T(8,128)S(1)}, u32[]{:S(2)}, u32[]{:S(2)}) collective-permute-start(f32[2,1,16,128]{3,2,1,0:T(8,128)S(1)} %slice.524), channel_id=1, source_target_pairs={{8,0},{16,8},{24,16},{9,1},{17,9},{25,17},{10,2},{18,10},{26,18},{... | collective-permute-start | bytes 49160 | tf_op jit(solution)/shard_map/ppermute | solution.py:27
  16.8 167.5 %all-to-all-start.1 = ((f32[1,192,8]{1,0,2:T(1,128)}), f32[1,192,8]{1,0,2:T(1,128)S(1)}, u32[]{:S(2)}, u32[]{:S(2)}) async-start(f32[1,192,8]{1,0,2:T(1,128)} %bitcast.109), calls=%async_computation.1 | async-start | bytes 16384 | tf_op jit(solution)/shard_map/all_to_all | solution.py:139
  25.6 20.6 %collective-permute-start.1 = (f32[2,4,16,1]{3,2,1,0:T(8,128)S(1)}, f32[2,4,16,1]{3,2,1,0:T(8,128)S(1)}, u32[]{:S(2)}, u32[]{:S(2)}) collective-permute-start(f32[2,4,16,1]{3,2,1,0:T(8,128)S(1)} %slice.518), channel_id=1, source_target_pairs={{1,0},{2,1},{3,2},{5,4},{6,5},{7,6},{9,8},{10,9},{11,10},{13,12},{... | collective-permute-start | bytes 1544 | tf_op jit(solution)/shard_map/ppermute | solution.py:27
  48.2 18.1 %collective-permute-start.3 = (f32[2,4,1,128]{3,2,1,0:T(1,128)S(1)}, f32[2,4,1,128]{3,2,1,0:T(1,128)S(1)}, u32[]{:S(2)}, u32[]{:S(2)}) collective-permute-start(f32[2,4,1,128]{3,2,1,0:T(1,128)S(1)} %slice.531), channel_id=1, source_target_pairs={{0,4},{1,5},{2,6},{3,7},{8,12},{9,13},{10,14},{11,15},{16,20},{17,... | collective-permute-start | bytes 12296 | tf_op jit(solution)/shard_map/ppermute | solution.py:27
  50.6 15.7 %collective-permute-start.5 = (f32[2,1,16,128]{3,2,1,0:T(8,128)S(1)}, f32[2,1,16,128]{3,2,1,0:T(8,128)S(1)}, u32[]{:S(2)}, u32[]{:S(2)}) collective-permute-start(f32[2,1,16,128]{3,2,1,0:T(8,128)S(1)} %slice.704), channel_id=1, source_target_pairs={{0,8},{8,16},{16,24},{1,9},{9,17},{17,25},{2,10},{10,18},{18,26},{... | collective-permute-start | bytes 49160 | tf_op jit(solution)/shard_map/ppermute | solution.py:27
  54.2 12.2 %collective-permute-start.4 = (f32[2,4,16,1]{3,2,1,0:T(8,128)S(1)}, f32[2,4,16,1]{3,2,1,0:T(8,128)S(1)}, u32[]{:S(2)}, u32[]{:S(2)}) collective-permute-start(f32[2,4,16,1]{3,2,1,0:T(8,128)S(1)} %slice.698), channel_id=1, source_target_pairs={{0,1},{1,2},{2,3},{4,5},{5,6},{6,7},{8,9},{9,10},{10,11},{12,13},{... | collective-permute-start | bytes 1544 | tf_op jit(solution)/shard_map/ppermute | solution.py:27
  66.7 11.8 %collective-permute-start.6 = (f32[2,4,1,128]{3,2,1,0:T(1,128)S(1)}, f32[2,4,1,128]{3,2,1,0:T(1,128)S(1)}, u32[]{:S(2)}, u32[]{:S(2)}) collective-permute-start(f32[2,4,1,128]{3,2,1,0:T(1,128)S(1)} %slice.556), channel_id=1, source_target_pairs={{4,0},{5,1},{6,2},{7,3},{12,8},{13,9},{14,10},{15,11},{20,16},{21,... | collective-permute-start | bytes 12296 | tf_op jit(solution)/shard_map/ppermute | solution.py:27
  68.0 10.6 %collective-permute-start.8 = (f32[2,1,16,128]{3,2,1,0:T(8,128)S(1)}, f32[2,1,16,128]{3,2,1,0:T(8,128)S(1)}, u32[]{:S(2)}, u32[]{:S(2)}) collective-permute-start(f32[2,1,16,128]{3,2,1,0:T(8,128)S(1)} %slice.722), channel_id=1, source_target_pairs={{8,0},{16,8},{24,16},{9,1},{17,9},{25,17},{10,2},{18,10},{26,18},{... | collective-permute-start | bytes 49160 | tf_op jit(solution)/shard_map/ppermute | solution.py:27
  69.3 9.2 %collective-permute-start.7 = (f32[2,4,16,1]{3,2,1,0:T(8,128)S(1)}, f32[2,4,16,1]{3,2,1,0:T(8,128)S(1)}, u32[]{:S(2)}, u32[]{:S(2)}) collective-permute-start(f32[2,4,16,1]{3,2,1,0:T(8,128)S(1)} %slice.716), channel_id=1, source_target_pairs={{1,0},{2,1},{3,2},{5,4},{6,5},{7,6},{9,8},{10,9},{11,10},{13,12},{... | collective-permute-start | bytes 1544 | tf_op jit(solution)/shard_map/ppermute | solution.py:27
  78.9 20.1 %collective-permute-start.9 = (f32[2,4,1,128]{3,2,1,0:T(1,128)S(1)}, f32[2,4,1,128]{3,2,1,0:T(1,128)S(1)}, u32[]{:S(2)}, u32[]{:S(2)}) collective-permute-start(f32[2,4,1,128]{3,2,1,0:T(1,128)S(1)} %slice.573), channel_id=1, source_target_pairs={{0,4},{1,5},{2,6},{3,7},{8,12},{9,13},{10,14},{11,15},{16,20},{17,... | collective-permute-start | bytes 12296 | tf_op jit(solution)/shard_map/ppermute | solution.py:27
  81.9 17.1 %collective-permute-start.11 = (f32[2,1,16,128]{3,2,1,0:T(8,128)S(1)}, f32[2,1,16,128]{3,2,1,0:T(8,128)S(1)}, u32[]{:S(2)}, u32[]{:S(2)}) collective-permute-start(f32[2,1,16,128]{3,2,1,0:T(8,128)S(1)} %slice.738), channel_id=1, source_target_pairs={{0,8},{8,16},{16,24},{1,9},{9,17},{17,25},{2,10},{10,18},{18,26},{... | collective-permute-start | bytes 49160 | tf_op jit(solution)/shard_map/ppermute | solution.py:27
  86.2 12.8 %collective-permute-start.10 = (f32[2,4,16,1]{3,2,1,0:T(8,128)S(1)}, f32[2,4,16,1]{3,2,1,0:T(8,128)S(1)}, u32[]{:S(2)}, u32[]{:S(2)}) collective-permute-start(f32[2,4,16,1]{3,2,1,0:T(8,128)S(1)} %slice.732), channel_id=1, source_target_pairs={{0,1},{1,2},{2,3},{4,5},{5,6},{6,7},{8,9},{9,10},{10,11},{12,13},{... | collective-permute-start | bytes 1544 | tf_op jit(solution)/shard_map/ppermute | solution.py:27
  99.3 11.8 %collective-permute-start.12 = (f32[2,4,1,128]{3,2,1,0:T(1,128)S(1)}, f32[2,4,1,128]{3,2,1,0:T(1,128)S(1)}, u32[]{:S(2)}, u32[]{:S(2)}) collective-permute-start(f32[2,4,1,128]{3,2,1,0:T(1,128)S(1)} %slice.592), channel_id=1, source_target_pairs={{4,0},{5,1},{6,2},{7,3},{12,8},{13,9},{14,10},{15,11},{20,16},{21,... | collective-permute-start | bytes 12296 | tf_op jit(solution)/shard_map/ppermute | solution.py:27
  100.6 10.6 %collective-permute-start.14 = (f32[2,1,16,128]{3,2,1,0:T(8,128)S(1)}, f32[2,1,16,128]{3,2,1,0:T(8,128)S(1)}, u32[]{:S(2)}, u32[]{:S(2)}) collective-permute-start(f32[2,1,16,128]{3,2,1,0:T(8,128)S(1)} %slice.756), channel_id=1, source_target_pairs={{8,0},{16,8},{24,16},{9,1},{17,9},{25,17},{10,2},{18,10},{26,18},{... | collective-permute-start | bytes 49160 | tf_op jit(solution)/shard_map/ppermute | solution.py:27
  111.5 20.4 %collective-permute-start.15 = (f32[2,4,1,128]{3,2,1,0:T(1,128)S(1)}, f32[2,4,1,128]{3,2,1,0:T(1,128)S(1)}, u32[]{:S(2)}, u32[]{:S(2)}) collective-permute-start(f32[2,4,1,128]{3,2,1,0:T(1,128)S(1)} %slice.609), channel_id=1, source_target_pairs={{0,4},{1,5},{2,6},{3,7},{8,12},{9,13},{10,14},{11,15},{16,20},{17,... | collective-permute-start | bytes 12296 | tf_op jit(solution)/shard_map/ppermute | solution.py:27
  114.5 17.3 %collective-permute-start.17 = (f32[2,1,16,128]{3,2,1,0:T(8,128)S(1)}, f32[2,1,16,128]{3,2,1,0:T(8,128)S(1)}, u32[]{:S(2)}, u32[]{:S(2)}) collective-permute-start(f32[2,1,16,128]{3,2,1,0:T(8,128)S(1)} %slice.772), channel_id=1, source_target_pairs={{0,8},{8,16},{16,24},{1,9},{9,17},{17,25},{2,10},{10,18},{18,26},{... | collective-permute-start | bytes 49160 | tf_op jit(solution)/shard_map/ppermute | solution.py:27
  118.8 13.0 %collective-permute-start.16 = (f32[2,4,16,1]{3,2,1,0:T(8,128)S(1)}, f32[2,4,16,1]{3,2,1,0:T(8,128)S(1)}, u32[]{:S(2)}, u32[]{:S(2)}) collective-permute-start(f32[2,4,16,1]{3,2,1,0:T(8,128)S(1)} %slice.766), channel_id=1, source_target_pairs={{0,1},{1,2},{2,3},{4,5},{5,6},{6,7},{8,9},{9,10},{10,11},{12,13},{... | collective-permute-start | bytes 1544 | tf_op jit(solution)/shard_map/ppermute | solution.py:27
  132.2 11.8 %collective-permute-start.18 = (f32[2,4,1,128]{3,2,1,0:T(1,128)S(1)}, f32[2,4,1,128]{3,2,1,0:T(1,128)S(1)}, u32[]{:S(2)}, u32[]{:S(2)}) collective-permute-start(f32[2,4,1,128]{3,2,1,0:T(1,128)S(1)} %slice.628), channel_id=1, source_target_pairs={{4,0},{5,1},{6,2},{7,3},{12,8},{13,9},{14,10},{15,11},{20,16},{21,... | collective-permute-start | bytes 12296 | tf_op jit(solution)/shard_map/ppermute | solution.py:27
  133.5 10.6 %collective-permute-start.20 = (f32[2,1,16,128]{3,2,1,0:T(8,128)S(1)}, f32[2,1,16,128]{3,2,1,0:T(8,128)S(1)}, u32[]{:S(2)}, u32[]{:S(2)}) collective-permute-start(f32[2,1,16,128]{3,2,1,0:T(8,128)S(1)} %slice.790), channel_id=1, source_target_pairs={{8,0},{16,8},{24,16},{9,1},{17,9},{25,17},{10,2},{18,10},{26,18},{... | collective-permute-start | bytes 49160 | tf_op jit(solution)/shard_map/ppermute | solution.py:27
  144.4 20.4 %collective-permute-start.21 = (f32[2,4,1,128]{3,2,1,0:T(1,128)S(1)}, f32[2,4,1,128]{3,2,1,0:T(1,128)S(1)}, u32[]{:S(2)}, u32[]{:S(2)}) collective-permute-start(f32[2,4,1,128]{3,2,1,0:T(1,128)S(1)} %slice.645), channel_id=1, source_target_pairs={{0,4},{1,5},{2,6},{3,7},{8,12},{9,13},{10,14},{11,15},{16,20},{17,... | collective-permute-start | bytes 12296 | tf_op jit(solution)/shard_map/ppermute | solution.py:27
  147.4 17.3 %collective-permute-start.23 = (f32[2,1,16,128]{3,2,1,0:T(8,128)S(1)}, f32[2,1,16,128]{3,2,1,0:T(8,128)S(1)}, u32[]{:S(2)}, u32[]{:S(2)}) collective-permute-start(f32[2,1,16,128]{3,2,1,0:T(8,128)S(1)} %slice.806), channel_id=1, source_target_pairs={{0,8},{8,16},{16,24},{1,9},{9,17},{17,25},{2,10},{10,18},{18,26},{... | collective-permute-start | bytes 49160 | tf_op jit(solution)/shard_map/ppermute | solution.py:27
  151.7 13.0 %collective-permute-start.22 = (f32[2,4,16,1]{3,2,1,0:T(8,128)S(1)}, f32[2,4,16,1]{3,2,1,0:T(8,128)S(1)}, u32[]{:S(2)}, u32[]{:S(2)}) collective-permute-start(f32[2,4,16,1]{3,2,1,0:T(8,128)S(1)} %slice.800), channel_id=1, source_target_pairs={{0,1},{1,2},{2,3},{4,5},{5,6},{6,7},{8,9},{9,10},{10,11},{12,13},{... | collective-permute-start | bytes 1544 | tf_op jit(solution)/shard_map/ppermute | solution.py:27
  184.3 9.3 %all-to-all-start = ((f32[8,3,192,1]{2,3,1,0:T(1,128)}), f32[8,3,192,1]{2,3,1,0:T(1,128)S(1)}, u32[]{:S(2)}, u32[]{:S(2)}) async-start(f32[8,3,192,1]{2,3,1,0:T(1,128)} %constant_dynamic-update-slice_fusion), calls=%async_computation | async-start | bytes 49152 | tf_op jit(solution)/shard_map/all_to_all | solution.py:16
  (7 other events, 172.8 us)
